TPU v7x, 512 devices: a whole 4x8x8 slice. The times are simulated.
512 devices in a mesh: ctx: 32 (over y, x), mp: 16 (over z, core).
Axes of the slice: x: 4, y: 8, z: 8, core: 2. Of those that a mesh axis runs over, the one named last changes fastest.
Arguments:
- source_rows: bfloat16 [16384, 3, 8192], P('ctx', None, 'mp'), may hold values from -6 to 6
- short_filters: bfloat16 [3, 7, 8192], P(None, None, 'mp'), may hold values from -2 to 2
- medium_filters: bfloat16 [128, 512], P(None, 'mp'), may hold values from -0.5 to 0.5
- skip_gain: float32 [8192], P('mp'), may hold values from 0.1 to 1.9
- out_weight: bfloat16 [8192, 8192], P('mp', 'ctx'), may hold values from -0.0625 to 0.0625
- doc_lengths: int32 [8], replicated, may hold values from 1 to 2048, 8192 in all
- block_packing_device: int32 [32, 16], replicated, may hold values from 0 to 31, as said below
Outputs:
- mixed: bfloat16 [8192, 8192], P('ctx', 'mp')
Inputs may be any that keep to these rules, and one draw needn't show every extreme that they name: `block_packing_device`: row c names, for the 16 blocks of stretch c in order, the packing device that holds each; the entries of one row differ, and some packing device is named in every row. A packing device keeps the blocks it holds in increasing order of their stretch, in its first slots.
All inputs are finite; a program needn't handle non-finite values.
Results may differ from a plain program's by a relative error of at most 0.02.
Values may be sent and summed in bfloat16 or wider, within the bound.
No kernel may reach another device: no remote copies, remote signals or barrier semaphores. Data moves between devices by JAX's collectives and lax.ppermute only.
A program may use at most 128 MiB of HBM per device.

v0:
```python
import jax
import jax.numpy as jnp
from jax import lax
from jax.sharding import PartitionSpec as P


def passed_along(block, axis, distance):
    devices = range(lax.axis_size(axis))
    route = [(i - distance, i) for i in devices if i - distance in devices]
    return lax.ppermute(block, axis, route)


def reach_back(positions, starts):
    begin = jnp.max(jnp.where(starts[None, :] <= positions[:, None], starts[None, :], 0), axis=1)
    return positions - begin


def short_conv(extended, filt, back, count):
    span = filt.shape[0]
    taps = filt.astype(jnp.float32)
    total = jnp.zeros((count, extended.shape[1]), jnp.float32)
    for step in range(span):
        keep = (back >= step).astype(jnp.float32)[:, None]
        piece = extended[span - 1 - step : span - 1 - step + count].astype(jnp.float32)
        total = total + taps[step][None, :] * piece * keep
    return total


def on_device(
    source_rows,
    short_filters,
    medium_filters,
    skip_gain,
    out_weight,
    doc_lengths,
    block_packing_device,
):
    stretches = lax.axis_size("ctx")
    rank_me = lax.axis_index("ctx")
    nb_own = block_packing_device.shape[1]
    blk = source_rows.shape[0] // stretches
    rows = nb_own * blk
    width = source_rows.shape[2]
    se_len = short_filters.shape[1]
    mr_len = medium_filters.shape[0]
    member = jnp.any(block_packing_device == rank_me, axis=1)
    flags = member.astype(jnp.int32)
    slots = jnp.cumsum(flags) - flags
    blocks = source_rows.reshape(stretches, blk, 3, width)
    outgoing = jnp.where(
        member[:, None, None, None], jnp.take(blocks, slots, axis=0), jnp.zeros((), jnp.bfloat16)
    )
    incoming = lax.all_to_all(outgoing, "ctx", split_axis=0, concat_axis=0, tiled=True)
    wanted = lax.dynamic_index_in_dim(block_packing_device, rank_me, 0, keepdims=False)
    stretch = jnp.take(incoming, wanted, axis=0).reshape(rows, 3, width)
    ends = jnp.cumsum(doc_lengths)
    starts = ends - doc_lengths
    base = rank_me * rows
    positions = base + jnp.arange(rows, dtype=jnp.int32)
    back = reach_back(positions, starts)
    span_cols = rows + mr_len - 1
    edge = stretch[rows - (se_len - 1) :]
    earlier = passed_along(edge, "ctx", 1)
    extended = jnp.concatenate([earlier, stretch], axis=0)
    query = short_conv(extended[:, 0], short_filters[0], back, rows)
    keyed = short_conv(extended[:, 1], short_filters[1], back, rows)
    valued = short_conv(extended[:, 2], short_filters[2], back, rows)
    z_vals = (keyed * valued).astype(jnp.bfloat16)
    z_prev = passed_along(z_vals[rows - (mr_len - 1) :], "ctx", 1)
    z_ext = jnp.concatenate([z_prev, z_vals], axis=0)
    groups_dev = medium_filters.shape[1]
    per_group = width // groups_dev
    reversed_taps = jnp.transpose(medium_filters[::-1])
    line = jnp.concatenate([reversed_taps, jnp.zeros((groups_dev, rows), jnp.bfloat16)], axis=1)
    band = jnp.tile(line, (1, rows + 1))[:, : rows * span_cols].reshape(groups_dev, rows, span_cols)
    ext_pos = base - (mr_len - 1) + jnp.arange(span_cols, dtype=jnp.int32)
    begin_rows = positions - back
    keep = ext_pos[None, :] >= begin_rows[:, None]
    band = jnp.where(keep[None, :, :], band, jnp.zeros((), jnp.bfloat16))
    medium = jnp.einsum(
        "gip,pgc->igc",
        band,
        z_ext.reshape(span_cols, groups_dev, per_group),
        preferred_element_type=jnp.float32,
    ).reshape(rows, width)
    hidden = (query * (medium + skip_gain[None, :] * z_vals.astype(jnp.float32))).astype(
        jnp.bfloat16
    )
    partial_value = jnp.dot(
        hidden,
        lax.all_gather(out_weight, "ctx", axis=1, tiled=True),
        preferred_element_type=jnp.float32,
    )
    return lax.psum_scatter(
        partial_value.astype(jnp.bfloat16), "mp", scatter_dimension=1, tiled=True
    )


def solution(mesh):
    return jax.shard_map(
        on_device,
        mesh=mesh,
        in_specs=(
            P("ctx", None, "mp"),
            P(None, None, "mp"),
            P(None, "mp"),
            P("mp"),
            P("mp", "ctx"),
            P(),
            P(),
        ),
        out_specs=P("ctx", "mp"),
        check_vma=False,
    )
```

profile of v0, /device:TPU:8, one launch (start us, length us, event | category | flops | bytes accessed | tf_op | source)
XLA Modules:
  0.0 223.9 jit_solution(3496047976561221424)
XLA Ops:
  6.5 0.0 copy-start
  6.5 0.0 all-gather.2.cloned.1.call-start
  6.5 0.7 all-gather.2.cloned.1.call-update
  7.3 0.7 compare_reduce_fusion
  8.0 0.1 copy.20
  8.1 0.1 reduce-window.14
  8.1 0.1 fusion.109
  8.3 0.0 copy-done
  8.3 0.6 gather_fusion
  8.9 0.0 copy-start.1
  8.9 0.0 copy-start.5
  9.0 0.0 copy-start.2
  9.0 1.5 select_select_fusion
  10.5 10.3 %all-to-all-start = ((bf16[32,16,3,512]{3,1,2,0:T(8,128)(2,1)}), bf16[32,16,3,512]{3,1,2,0:T(8,128)(2,1)S(1)}, u32[]{:S(2)}, u32[]{:S(2)}) async-start(bf16[32,16,3,512]{3,1,2,0:T(8,128)(2,1)} %select_select_fusion), calls=%async_computation | async-start | bytes 3145728 | tf_op jit(solution)/shard_map/all_to_all | solution.py:53
  20.8 0.0 reduce-scatter.2.cloned.1.call-start
  20.9 0.0 copy-done.1
  20.9 0.2 dynamic-slice_reduce_fusion
  21.1 0.1 broadcast_in_dim.54
  21.1 0.1 broadcast_in_dim.55
  21.2 0.0 copy-done.5
  21.2 0.2 reduce-window.15
  21.5 0.1 select_reduce_fusion
  21.6 0.0 copy-done.2
  21.6 0.6 fusion.111
  22.2 42.6 %all-to-all-done = bf16[32,16,3,512]{3,1,2,0:T(8,128)(2,1)S(1)} async-done(((bf16[32,16,3,512]{3,1,2,0:T(8,128)(2,1)}), bf16[32,16,3,512]{3,1,2,0:T(8,128)(2,1)S(1)}, u32[]{:S(2)}, u32[]{:S(2)}) %all-to-all-start) | async-done | bytes 1572896 | tf_op jit(solution)/shard_map/all_to_all | solution.py:53
  64.8 1.5 gather_fusion.1
  66.4 1.2 copy.22
  67.6 0.2 bitcast_select_fusion
  67.8 3.3 %collective-permute-start = (bf16[6,3,512]{2,0,1:T(8,128)(2,1)S(1)}, bf16[6,3,512]{2,0,1:T(8,128)(2,1)S(1)}, u32[]{:S(2)}, u32[]{:S(2)}) collective-permute-start(bf16[6,3,512]{2,0,1:T(8,128)(2,1)S(1)} %slice.268), channel_id=1, source_target_pairs={{0,16},{16,32},{32,48},{48,64},{64,80},{80,96},{96,112},{112,128},... | collective-permute-start | bytes 55304 | tf_op jit(solution)/shard_map/ppermute | solution.py:10
  71.0 0.0 copy-done.3
  71.0 0.1 rev.3
  71.1 0.6 tile.4
  71.7 0.8 copy.25
  72.5 3.0 %slice.325 = bf16[32,98048]{1,0:T(8,128)(2,1)} slice(bf16[32,98688]{1,0:T(8,128)(2,1)S(1)} %bitcast.156), slice={[0:32], [0:98048]} | slice | bytes 12550144 | tf_op jit(solution)/shard_map/slice | solution.py:75
  75.5 18.4 %reshape.310 = bf16[32,256,383]{2,1,0:T(8,128)(2,1)} reshape(bf16[32,98048]{1,0:T(8,128)(2,1)} %slice.325) | data formatting | bytes 12550144 | tf_op jit(solution)/shard_map/reshape | solution.py:75
  93.9 0.0 collective-permute-done
  93.9 1.6 fusion.7
  95.5 3.8 %collective-permute-start.1 = (bf16[127,512]{1,0:T(8,128)(2,1)S(1)}, bf16[127,512]{1,0:T(8,128)(2,1)S(1)}, u32[]{:S(2)}, u32[]{:S(2)}) collective-permute-start(bf16[127,512]{1,0:T(8,128)(2,1)S(1)} %slice.324), channel_id=1, source_target_pairs={{0,16},{16,32},{32,48},{48,64},{64,80},{80,96},{96,112},{112,128},... | collective-permute-start | bytes 390152 | tf_op jit(solution)/shard_map/ppermute | solution.py:10
  99.3 0.1 broadcast_compare_fusion
  99.5 7.9 %collective-permute-done.1 = bf16[127,512]{1,0:T(8,128)(2,1)S(1)} collective-permute-done((bf16[127,512]{1,0:T(8,128)(2,1)S(1)}, bf16[127,512]{1,0:T(8,128)(2,1)S(1)}, u32[]{:S(2)}, u32[]{:S(2)}) %collective-permute-start.1) | collective-permute-done | bytes 130080 | tf_op jit(solution)/shard_map/ppermute | solution.py:10
  107.3 0.1 pad_maximum_fusion
  107.4 0.2 copy.23
  107.6 5.5 %fusion = f32[32,16,256]{2,1,0:T(8,128)} fusion(bf16[383,32,16]{0,2,1:T(8,128)(2,1)S(1)} %bitcast.158, bf16[32,256,383]{2,1,0:T(8,128)(2,1)} %reshape.310, pred[256,383]{1,0:T(8,128)(4,1)S(1)} %broadcast_compare_fusion), kind=kOutput, calls=%fused_computation.3 | convolution fusion | flops 103538688 | bytes 7289600 | tf_op jit(solution)/shard_map/gip,pgc->igc/dot_general | solution.py:80
  113.1 1.2 copy.24
  114.4 26.8 %all-gather.2.cloned.1.call-done = bf16[512,8192]{1,0:T(8,128)(2,1)} async-done(((bf16[512,256]{1,0:T(8,128)(2,1)}), bf16[512,8192]{1,0:T(8,128)(2,1)}) %all-gather.2.cloned.1.call-update) | async-done | bytes 8388624 | tf_op jit(solution)/shard_map/all_gather | solution.py:91
  141.1 8.1 %convolution_convert_fusion = bf16[256,8192]{1,0:T(8,128)(2,1)} fusion(bf16[512,8192]{1,0:T(8,128)(2,1)} %all-gather.2.cloned.1.call-done, f32[256,512]{1,0:T(8,128)S(1)} %copy.24, bf16[256,512]{1,0:T(8,128)(2,1)S(1)} %fusion.7, bf16[6,3,512]{2,0,1:T(8,128)(2,1)S(1)} %collective-permute-done, bf16[256,3,512]{2,0,1:T(8,128)(2,1)S(1)} %bitcast_select_fusion, ...), kind=kOutput, calls=%fused_computation.2 | convolution fusion | flops 2156920832 | bytes 14466048 | tf_op jit(solution)/shard_map/dot_general | solution.py:89
  149.2 0.0 reduce-scatter.2.cloned.1.call-update
  149.2 67.8 %reduce-scatter.2.cloned.1.call-done = bf16[256,512]{1,0:T(8,128)(2,1)} async-done(((bf16[256,8192]{1,0:T(8,128)(2,1)}), bf16[256,512]{1,0:T(8,128)(2,1)}) %reduce-scatter.2.cloned.1.call-update) | async-done | bytes 262160 | tf_op jit(solution)/shard_map/reduce_scatter | solution.py:94
  (19 shorter events, 0.2 us)
Async XLA Ops:
  6.5 1.7 copy-start
  6.5 134.6 %all-gather.2.cloned.1.call-start = ((), (), s32[]{:S(2)}) async-start(), calls=%async_computation.2 | async-start | bytes 8650752 | tf_op jit(solution)/shard_map/all_gather | solution.py:91
  8.9 11.9 %copy-start.1 = (s32[32,16]{0,1:T(8,128)S(1)}, s32[32,16]{0,1:T(8,128)}, u32[]{:S(2)}) copy-start(s32[32,16]{0,1:T(8,128)} %param.13) | copy-start | bytes 6148
  8.9 12.3 %copy-start.5 = (s32[8]{0:T(128)S(1)}, s32[8]{0:T(128)}, u32[]{:S(2)}) copy-start(s32[8]{0:T(128)} %param.12) | copy-start | bytes 100
  9.0 12.6 %copy-start.2 = (bf16[3,7,512]{2,1,0:T(8,128)(2,1)S(1)}, bf16[3,7,512]{2,1,0:T(8,128)(2,1)}, u32[]{:S(2)}) copy-start(bf16[3,7,512]{2,1,0:T(8,128)(2,1)} %param.8) | copy-start | bytes 64516
  10.5 60.5 %copy-start.3 = (bf16[128,32]{0,1:T(8,128)(2,1)S(1)}, bf16[128,32]{0,1:T(8,128)(2,1)}, u32[]{:S(2)}) copy-start(bf16[128,32]{0,1:T(8,128)(2,1)} %param.9) | copy-start | bytes 24580
  10.5 54.3 %all-to-all-start = ((bf16[32,16,3,512]{3,1,2,0:T(8,128)(2,1)}), bf16[32,16,3,512]{3,1,2,0:T(8,128)(2,1)S(1)}, u32[]{:S(2)}, u32[]{:S(2)}) async-start(bf16[32,16,3,512]{3,1,2,0:T(8,128)(2,1)} %select_select_fusion), calls=%async_computation | async-start | bytes 3145728 | tf_op jit(solution)/shard_map/all_to_all | solution.py:53
  20.8 196.2 %reduce-scatter.2.cloned.1.call-start = ((), (), s32[]{:S(2)}) async-start(), calls=%async_computation.3 | async-start | bytes 4456448 | tf_op jit(solution)/shard_map/reduce_scatter | solution.py:94
  21.6 72.3 %copy-start.4 = (f32[256]{0:T(256)}, f32[256]{0:T(256)S(1)}, u32[]{:S(2)}) copy-start(f32[256]{0:T(256)S(1)} %get-tuple-element.38) | copy-start | bytes 3076
  67.8 26.1 %collective-permute-start = (bf16[6,3,512]{2,0,1:T(8,128)(2,1)S(1)}, bf16[6,3,512]{2,0,1:T(8,128)(2,1)S(1)}, u32[]{:S(2)}, u32[]{:S(2)}) collective-permute-start(bf16[6,3,512]{2,0,1:T(8,128)(2,1)S(1)} %slice.268), channel_id=1, source_target_pairs={{0,16},{16,32},{32,48},{48,64},{64,80},{80,96},{96,112},{112,128},... | collective-permute-start | bytes 55304 | tf_op jit(solution)/shard_map/ppermute | solution.py:10
  95.5 11.8 %collective-permute-start.1 = (bf16[127,512]{1,0:T(8,128)(2,1)S(1)}, bf16[127,512]{1,0:T(8,128)(2,1)S(1)}, u32[]{:S(2)}, u32[]{:S(2)}) collective-permute-start(bf16[127,512]{1,0:T(8,128)(2,1)S(1)} %slice.324), channel_id=1, source_target_pairs={{0,16},{16,32},{32,48},{48,64},{64,80},{80,96},{96,112},{112,128},... | collective-permute-start | bytes 390152 | tf_op jit(solution)/shard_map/ppermute | solution.py:10
Sparse Core Ops, SparseCore 0:
  10.4 130.6 all-gather.1
  149.4 67.6 reduce-scatter.1
where the time goes:
time: 224 us
  waiting for transfers between devices  146 us (65%)
  local copies, waits for them, and re-layouts  28.8 us (13%)
  starting transfers between devices  17.4 us (8%)
  matrix products  13.6 us (6%)
  between operations  13.6 us (6%)
  other arithmetic  4.66 us (2%)
    reduce_scatter x1, waiting for transfers between devices, on_device(): lax.psum_scatter(partial_value.astype(jnp.bfloat16), 'mp', scatter_dimens...  67.8 us
    all_to_all x1, waiting for transfers between devices, on_device(): lax.all_to_all(outgoing, 'ctx', split_axis=0, concat_axis=0, tiled=True)  42.6 us
    all_gather x1, waiting for transfers between devices, on_device(): lax.all_gather(out_weight, 'ctx', axis=1, tiled=True)  26.8 us
    reshape x1, local copies, waits for them, and re-layouts, on_device(): jnp.tile(line, (1, rows + 1))[:, :rows * span_cols]  18.4 us
    all_to_all x1, starting transfers between devices, on_device(): lax.all_to_all(outgoing, 'ctx', split_axis=0, concat_axis=0, tiled=True)  10.3 us
    dot_general x1, matrix products, on_device(): jnp.dot(hidden, lax.all_gather(out_weight, 'ctx', axis=1, tiled=True), pr...  8.11 us
    ppermute x2, waiting for transfers between devices, passed_along(): return lax.ppermute(block, axis, route)  7.88 us
    ppermute x2, starting transfers between devices, passed_along(): return lax.ppermute(block, axis, route)  7.08 us
  transfers between devices with their start and end apart: 5, of which 4 were waited for; matrix products, arithmetic and copies ran while one was open for 17% of the time, Pallas kernels for 0%

commit v1 on v0

--- a/solution.py
+++ b/solution.py
@@ -2,6 +2,11 @@
 import jax.numpy as jnp
 from jax import lax
 from jax.sharding import PartitionSpec as P
+
+
+def swapped_in(shard, axis, along):
+    sent = jnp.stack([shard] * lax.axis_size(axis))
+    return jnp.concatenate(lax.all_to_all(sent, axis, 0, 0), axis=along)
 
 
 def passed_along(block, axis, distance):
@@ -87,9 +92,7 @@
         jnp.bfloat16
     )
     partial_value = jnp.dot(
-        hidden,
-        lax.all_gather(out_weight, "ctx", axis=1, tiled=True),
-        preferred_element_type=jnp.float32,
+        hidden, swapped_in(out_weight, "ctx", 1), preferred_element_type=jnp.float32
     )
     return lax.psum_scatter(
         partial_value.astype(jnp.bfloat16), "mp", scatter_dimension=1, tiled=True

time: 224 us -> 359 us (1.60)
  the two profiles are of different devices: /device:TPU:8 before, /device:TPU:6 now
where the time goes in v1:
time: 359 us; the launch traced here: 358 us
  waiting for transfers between devices  265 us (74%)
  local copies, waits for them, and re-layouts  33.5 us (9%)
  starting transfers between devices  26 us (7%)
  matrix products  14.4 us (4%)
  between operations  13.6 us (4%)
  other arithmetic  5.35 us (1%)
    ppermute x2, waiting for transfers between devices, passed_along(): return lax.ppermute(block, axis, route)  155 us
    reduce_scatter x1, waiting for transfers between devices, on_device(): lax.psum_scatter(partial_value.astype(jnp.bfloat16), 'mp', scatter_dimens...  72.4 us
    all_to_all x1, waiting for transfers between devices, on_device(): lax.all_to_all(outgoing, 'ctx', split_axis=0, concat_axis=0, tiled=True)  38.2 us
    reshape x1, local copies, waits for them, and re-layouts, on_device(): jnp.tile(line, (1, rows + 1))[:, :rows * span_cols]  18.4 us
    all_to_all x1, starting transfers between devices, on_device(): lax.all_to_all(outgoing, 'ctx', split_axis=0, concat_axis=0, tiled=True)  10.2 us
    ppermute x2, starting transfers between devices, passed_along(): return lax.ppermute(block, axis, route)  10.1 us
    dot_general x1, matrix products, on_device(): jnp.dot(hidden, swapped_in(out_weight, 'ctx', 1), preferred_element_type=...  9.77 us
  transfers between devices with their start and end apart: 5, of which 4 were waited for; matrix products, arithmetic and copies ran while one was open for 10% of the time, Pallas kernels for 0%

profile of v1, /device:TPU:6, one launch (start us, length us, event | category | flops | bytes accessed | tf_op | source)
XLA Modules:
  0.0 358.1 jit_solution(443335233735151962)
XLA Ops:
  6.5 0.0 copy-start
  6.5 0.8 compare_reduce_fusion
  7.4 0.1 copy.22
  7.5 0.1 reduce-window.14
  7.5 0.1 fusion.139
  7.7 0.3 copy-done
  8.0 0.6 gather_fusion
  8.6 1.4 select_select_fusion
  10.0 10.2 %all-to-all-start = ((bf16[32,16,3,512]{3,1,2,0:T(8,128)(2,1)}), bf16[32,16,3,512]{3,1,2,0:T(8,128)(2,1)S(1)}, u32[]{:S(2)}, u32[]{:S(2)}) async-start(bf16[32,16,3,512]{3,1,2,0:T(8,128)(2,1)} %select_select_fusion), calls=%async_computation | async-start | bytes 3145728 | tf_op jit(solution)/shard_map/all_to_all | solution.py:58
  20.2 1.1 copy.27
  21.3 38.2 %all-to-all-done = bf16[32,16,3,512]{3,1,2,0:T(8,128)(2,1)S(1)} async-done(((bf16[32,16,3,512]{3,1,2,0:T(8,128)(2,1)}), bf16[32,16,3,512]{3,1,2,0:T(8,128)(2,1)S(1)}, u32[]{:S(2)}, u32[]{:S(2)}) %all-to-all-start) | async-done | bytes 1572896 | tf_op jit(solution)/shard_map/all_to_all | solution.py:58
  59.5 4.2 %stack.2 = bf16[32,512,256]{1,2,0:T(8,128)(2,1)} broadcast(bf16[512,256]{0,1:T(8,128)(2,1)S(1)} %copy.27), dimensions={1,2} | broadcast | bytes 8650752 | tf_op jit(solution)/shard_map/stack | solution.py:8
  63.7 0.0 copy-start.5
  63.7 5.8 %all-to-all-start.1 = ((bf16[32,512,256]{1,2,0:T(8,128)(2,1)}), bf16[32,512,256]{1,2,0:T(8,128)(2,1)}, u32[]{:S(2)}, u32[]{:S(2)}) async-start(bf16[32,512,256]{1,2,0:T(8,128)(2,1)} %stack.2), calls=%async_computation.1 | async-start | bytes 16777216 | tf_op jit(solution)/shard_map/all_to_all | solution.py:9
  69.5 0.0 copy-start.3
  69.5 0.0 reduce-scatter.2.cloned.1.call-start
  69.5 0.0 copy-done.5
  69.5 0.2 reduce-window.15
  69.7 0.0 copy-done.1
  69.7 0.2 dynamic-slice_reduce_fusion
  69.9 0.1 broadcast_in_dim.54
  70.0 0.1 broadcast_in_dim.55
  70.1 0.1 select_reduce_fusion
  70.2 0.0 copy-done.2
  70.3 1.5 gather_fusion.1
  71.8 1.2 copy.24
  73.0 0.2 bitcast_select_fusion
  73.2 3.4 collective-permute-start
  76.6 0.0 copy-done.3
  76.6 0.1 rev.3
  76.7 0.6 tile.4
  77.3 0.8 copy.28
  78.1 3.0 slice.346
  81.1 18.4 %reshape.563 = bf16[32,256,383]{2,1,0:T(8,128)(2,1)} reshape(bf16[32,98048]{1,0:T(8,128)(2,1)} %slice.346) | data formatting | bytes 12550144 | tf_op jit(solution)/shard_map/reshape | solution.py:80
  99.5 152.4 %collective-permute-done = bf16[6,3,512]{2,0,1:T(8,128)(2,1)S(1)} collective-permute-done((bf16[6,3,512]{2,0,1:T(8,128)(2,1)S(1)}, bf16[6,3,512]{2,0,1:T(8,128)(2,1)S(1)}, u32[]{:S(2)}, u32[]{:S(2)}) %collective-permute-start) | collective-permute-done | bytes 18464 | tf_op jit(solution)/shard_map/ppermute | solution.py:15
  251.9 2.2 fusion.13
  254.2 6.7 %collective-permute-start.1 = (bf16[127,512]{1,0:T(8,128)(2,1)S(1)}, bf16[127,512]{1,0:T(8,128)(2,1)S(1)}, u32[]{:S(2)}, u32[]{:S(2)}) collective-permute-start(bf16[127,512]{1,0:T(8,128)(2,1)S(1)} %slice.345), channel_id=1, source_target_pairs={{0,16},{16,32},{32,48},{48,64},{64,80},{80,96},{96,112},{112,128},... | collective-permute-start | bytes 390152 | tf_op jit(solution)/shard_map/ppermute | solution.py:15
  260.8 0.1 broadcast_compare_fusion
  261.0 2.2 collective-permute-done.1
  263.2 0.1 pad_maximum_fusion
  263.2 0.9 copy.25
  264.2 4.7 %fusion = f32[32,16,256]{2,1,0:T(8,128)S(1)} fusion(bf16[383,32,16]{0,2,1:T(8,128)(2,1)} %bitcast.190, bf16[32,256,383]{2,1,0:T(8,128)(2,1)} %reshape.563, pred[256,383]{1,0:T(8,128)(4,1)S(1)} %broadcast_compare_fusion), kind=kOutput, calls=%fused_computation.3 | convolution fusion | flops 103538688 | bytes 7289600 | tf_op jit(solution)/shard_map/gip,pgc->igc/dot_general | solution.py:85
  268.8 0.2 copy.26
  269.1 0.0 all-to-all-done.1
  269.1 0.0 copy-done.4
  269.1 9.8 %convolution_convert_fusion = bf16[256,8192]{1,0:T(8,128)(2,1)} fusion(bf16[512,8192]{0,1:T(8,128)(2,1)} %bitcast.47, f32[256,1,512]{2,0,1:T(8,128)S(1)} %copy.26, bf16[6,3,512]{2,0,1:T(8,128)(2,1)S(1)} %collective-permute-done, bf16[256,3,512]{2,0,1:T(8,128)(2,1)S(1)} %bitcast_select_fusion, bf16[256,1,512]{2,0,1:T(8,128)(2,1)} %get-tuple-element.8, ...), kind=kOutput, calls=%fused_computation.2 | convolution fusion | flops 2167799808 | bytes 15019008 | tf_op jit(solution)/shard_map/dot_general | solution.py:94
  278.9 0.0 reduce-scatter.2.cloned.1.call-update
  278.9 72.4 %reduce-scatter.2.cloned.1.call-done = bf16[256,512]{1,0:T(8,128)(2,1)} async-done(((bf16[256,8192]{1,0:T(8,128)(2,1)}), bf16[256,512]{1,0:T(8,128)(2,1)}) %reduce-scatter.2.cloned.1.call-update) | async-done | bytes 262160 | tf_op jit(solution)/shard_map/reduce_scatter | solution.py:97
  (20 shorter events, 0.2 us)
Async XLA Ops:
  6.5 1.4 copy-start
  10.0 49.5 %all-to-all-start = ((bf16[32,16,3,512]{3,1,2,0:T(8,128)(2,1)}), bf16[32,16,3,512]{3,1,2,0:T(8,128)(2,1)S(1)}, u32[]{:S(2)}, u32[]{:S(2)}) async-start(bf16[32,16,3,512]{3,1,2,0:T(8,128)(2,1)} %select_select_fusion), calls=%async_computation | async-start | bytes 3145728 | tf_op jit(solution)/shard_map/all_to_all | solution.py:58
  63.7 5.8 %copy-start.5 = (s32[8]{0:T(128)S(1)}, s32[8]{0:T(128)}, u32[]{:S(2)}) copy-start(s32[8]{0:T(128)} %param.12) | copy-start | bytes 100
  63.7 6.0 %copy-start.1 = (s32[32,16]{0,1:T(8,128)S(1)}, s32[32,16]{0,1:T(8,128)}, u32[]{:S(2)}) copy-start(s32[32,16]{0,1:T(8,128)} %param.13) | copy-start | bytes 6148
  63.7 6.5 %copy-start.2 = (bf16[3,7,512]{2,1,0:T(8,128)(2,1)S(1)}, bf16[3,7,512]{2,1,0:T(8,128)(2,1)}, u32[]{:S(2)}) copy-start(bf16[3,7,512]{2,1,0:T(8,128)(2,1)} %param.8) | copy-start | bytes 64516
  63.7 205.4 %all-to-all-start.1 = ((bf16[32,512,256]{1,2,0:T(8,128)(2,1)}), bf16[32,512,256]{1,2,0:T(8,128)(2,1)}, u32[]{:S(2)}, u32[]{:S(2)}) async-start(bf16[32,512,256]{1,2,0:T(8,128)(2,1)} %stack.2), calls=%async_computation.1 | async-start | bytes 16777216 | tf_op jit(solution)/shard_map/all_to_all | solution.py:9
  69.5 7.1 %copy-start.3 = (bf16[128,32]{0,1:T(8,128)(2,1)S(1)}, bf16[128,32]{0,1:T(8,128)(2,1)}, u32[]{:S(2)}) copy-start(bf16[128,32]{0,1:T(8,128)(2,1)} %param.9) | copy-start | bytes 24580
  69.5 281.8 %reduce-scatter.2.cloned.1.call-start = ((), (), s32[]{:S(2)}) async-start(), calls=%async_computation.3 | async-start | bytes 4456448 | tf_op jit(solution)/shard_map/reduce_scatter | solution.py:97
  73.2 178.7 %collective-permute-start = (bf16[6,3,512]{2,0,1:T(8,128)(2,1)S(1)}, bf16[6,3,512]{2,0,1:T(8,128)(2,1)S(1)}, u32[]{:S(2)}, u32[]{:S(2)}) collective-permute-start(bf16[6,3,512]{2,0,1:T(8,128)(2,1)S(1)} %slice.289), channel_id=1, source_target_pairs={{0,16},{16,32},{32,48},{48,64},{64,80},{80,96},{96,112},{112,128},... | collective-permute-start | bytes 55304 | tf_op jit(solution)/shard_map/ppermute | solution.py:15
  254.2 9.0 %collective-permute-start.1 = (bf16[127,512]{1,0:T(8,128)(2,1)S(1)}, bf16[127,512]{1,0:T(8,128)(2,1)S(1)}, u32[]{:S(2)}, u32[]{:S(2)}) collective-permute-start(bf16[127,512]{1,0:T(8,128)(2,1)S(1)} %slice.345), channel_id=1, source_target_pairs={{0,16},{16,32},{32,48},{48,64},{64,80},{80,96},{96,112},{112,128},... | collective-permute-start | bytes 390152 | tf_op jit(solution)/shard_map/ppermute | solution.py:15
  264.2 4.9 %copy-start.4 = (f32[512]{0:T(512)S(1)}, f32[512]{0:T(512)}, u32[]{:S(2)}) copy-start(f32[512]{0:T(512)} %param.10) | copy-start | bytes 6148
Sparse Core Ops, SparseCore 0:
  279.0 72.2 reduce-scatter.1
